TPU v7x, 32 devices: a whole 2x2x4 slice. The times are simulated.
32 devices in a mesh: fsdp: 8 (over y, x, core), mode: 4 (over z).
Axes of the slice: x: 2, y: 2, z: 4, core: 2. Of those that a mesh axis runs over, the one named last changes fastest.
Arguments:
- gradient: float32 [32, 16, 2, 256, 512], P('mode', None, None, 'fsdp'), may hold values from -1000 to 1000, as said below
- start_in: float32 [512, 128], replicated, may hold values from -6 to 6
- start_out: float32 [256, 128], replicated, may hold values from -6 to 6
- start_x: float32 [32, 16], replicated, may hold values from -6 to 6
- start_y: float32 [16, 8], replicated, may hold values from -6 to 6
Outputs:
- factor_in: float32 [512, 128], P(('fsdp', 'mode'))
- factor_out: float32 [256, 128], P('fsdp')
- factor_x: float32 [32, 16], replicated
- factor_y: float32 [16, 8], replicated
- core: float32 [16, 128, 8, 2, 128], P('mode', 'fsdp')
Inputs may be any that keep to these rules, and one draw needn't show every extreme that they name: A weight gradient of one spectral layer, finite and bounded in magnitude.
All inputs are finite; a program needn't handle non-finite values.
Results may differ from a plain program's by a relative error of at most 0.0003.
Values sent between devices are 32-bit elements; how exact they have to be, the bound alone decides.
No kernel may reach another device: no remote copies, remote signals or barrier semaphores. Data moves between devices by JAX's collectives and lax.ppermute only.
A program may use at most 320 MiB of HBM per device.

v0:
```python
import jax
import jax.numpy as jnp
from jax import lax
from jax.sharding import PartitionSpec as P

I = 512
SWEEPS = 2
precise = lax.Precision.HIGHEST


def sweeps(gram, subspace):
    for sweep_index in range(SWEEPS):
        product = jnp.dot(gram, subspace, precision=precise)
        inner = jnp.dot(product.T, product, precision=precise)
        lower_factor = jnp.linalg.cholesky(inner)
        subspace = jax.scipy.linalg.solve_triangular(lower_factor, product.T, lower=True).T
    return subspace


def shards(gradient, start_in, start_out, start_x, start_y):
    fsdp_index = lax.axis_index("fsdp")
    mode_index = lax.axis_index("mode")
    joint_index = lax.axis_index(("fsdp", "mode"))
    fsdp_count = lax.axis_size("fsdp")
    mode_count = lax.axis_size("mode")
    rows_in = I // (fsdp_count * mode_count)
    local_first = gradient.shape[0]
    local_out = gradient.shape[3]
    gram_y_part = jnp.einsum("xycoi,xzcoi->yz", gradient, gradient, precision=precise)
    gram_in_part = jnp.einsum("xycoi,xycoj->ij", gradient, gradient, precision=precise)
    gram_in, gram_y = lax.psum((gram_in_part, gram_y_part), ("fsdp", "mode"))
    full_in = sweeps(gram_in, start_in)
    factor_y = sweeps(gram_y, start_y)
    by_out = lax.all_to_all(gradient, "fsdp", split_axis=4, concat_axis=3, tiled=True)
    gram_out = lax.psum(
        jnp.einsum("xycoi,xycpi->op", by_out, by_out, precision=precise), ("fsdp", "mode")
    )
    by_first = lax.all_to_all(gradient, "mode", split_axis=4, concat_axis=0, tiled=True)
    gram_x = lax.psum(
        jnp.einsum("xycoi,zycoi->xz", by_first, by_first, precision=precise), ("fsdp", "mode")
    )
    full_out = sweeps(gram_out, start_out)
    factor_x = sweeps(gram_x, start_x)
    partial_in = jnp.einsum("xycoi,ia->xycoa", gradient, full_in, precision=precise)
    out_rows = lax.dynamic_slice_in_dim(full_out, fsdp_index * local_out, local_out, 0)
    first_rows = lax.dynamic_slice_in_dim(factor_x, mode_index * local_first, local_first, 0)
    reduced = jnp.einsum("xycoa,yq->xqcoa", partial_in, factor_y, precision=precise)
    columns = first_rows
    partial_core = lax.psum_scatter(
        jnp.einsum("xqcoa,xp->pqcoa", reduced, columns, precision=precise),
        "mode",
        scatter_dimension=0,
        tiled=True,
    )
    columns = out_rows
    swapped = lax.psum_scatter(
        jnp.einsum("pqcoa,ob->bpqca", partial_core, columns, precision=precise),
        "fsdp",
        scatter_dimension=0,
        tiled=True,
    )
    core = jnp.transpose(swapped, (1, 0, 2, 3, 4))
    factor_in = lax.dynamic_slice_in_dim(full_in, joint_index * rows_in, rows_in, 0)
    return (factor_in, out_rows, factor_x, factor_y, core)


def solution(mesh):
    in_specs = (P("mode", None, None, "fsdp", None), P(), P(), P(), P())
    out_specs = (
        P(("fsdp", "mode"), None),
        P("fsdp", None),
        P(),
        P(),
        P("mode", "fsdp", None, None, None),
    )
    return jax.shard_map(shards, mesh=mesh, in_specs=in_specs, out_specs=out_specs, check_vma=False)
```

profile of v0, /device:TPU:0, one launch (start us, length us, event | category | flops | bytes accessed | tf_op | source)
XLA Modules:
  0.0 1270.9 jit_solution(15433066055648959006)
XLA Ops:
  7.2 50.4 %copy.78 = f32[8,16,2,32,512]{3,1,2,0,4:T(8,128)} copy(f32[8,16,2,32,512]{4,3,2,1,0:T(8,128)} %param.16) | data formatting | bytes 33554432 | tf_op args[0]
  57.6 67.0 %reshape.45 = f32[8,1,524288]{2,1,0:T(1,128)} reshape(f32[512,8,2,16,32]{4,3,2,1,0:T(8,128)} %bitcast.156) | data formatting | bytes 33554432
  130.3 60.2 %reshape.47 = f32[4,1,1048576]{2,1,0:T(1,128)} reshape(f32[512,8,2,16,32]{4,3,2,1,0:T(8,128)} %bitcast.158) | data formatting | bytes 33554432
  190.5 124.4 %all-to-all-done = f32[8,1,524288]{2,1,0:T(1,128)} async-done(((f32[8,1,524288]{2,1,0:T(1,128)}), f32[8,1,524288]{2,1,0:T(1,128)}, u32[]{:S(2)}, u32[]{:S(2)}) %all-to-all-start) | async-done | bytes 16777248 | tf_op jit(solution)/shard_map/all_to_all | solution.py:34
  322.2 31.6 %fusion.13 = f32[512,512]{1,0:T(8,128)} fusion(f32[8,16,2,32,512]{4,3,2,1,0:T(8,128)} %param.16), kind=kOutput, calls=%fused_computation.12 | convolution fusion | flops 25769803776 | bytes 17825792 | tf_op jit(solution)/shard_map/xycoi,xycoj->ij/dot_general | solution.py:30
  354.3 50.6 %reduce.12 = f32[8,524288]{1,0:T(8,128)} reduce(f32[8,1,524288]{2,1,0:T(1,128)} %all-to-all-done, f32[]{:T(128)} %broadcast.120), dimensions={1}, to_apply=%all_to_all.26.reduce_sub_computation | reduce | bytes 33554436 | tf_op jit(solution)/shard_map/all_to_all | solution.py:34
  404.9 55.4 %reshape.46 = f32[512,8,2,16,32]{4,3,2,1,0:T(8,128)} reshape(f32[8,524288]{1,0:T(8,128)} %reduce.12) | data formatting | bytes 33554432
  460.3 48.4 %copy.113 = f32[8,16,2,32,8,64]{5,3,4,1,0,2:T(8,128)} copy(f32[8,16,2,32,8,64]{3,1,2,0,5,4:T(8,128)} %bitcast.11) | data formatting | bytes 33554432 | tf_op jit(solution)/shard_map/all_to_all | solution.py:34
  508.7 36.8 %convolution_bitcast_fusion.1 = f32[256,256]{1,0:T(8,128)} fusion(f32[8,16,2,256,64]{4,3,1,0,2:T(8,128)} %bitcast.196), kind=kOutput, calls=%fused_computation.13 | convolution fusion | flops 12884901888 | bytes 17039360 | tf_op jit(solution)/shard_map/xycoi,xycpi->op/dot_general | solution.py:36
  545.6 51.9 %fusion.19 = f32[16,16]{1,0:T(8,128)S(1)} fusion(f32[8,16,2,32,512]{4,3,2,1,0:T(8,128)} %param.16), kind=kOutput, calls=%fused_computation.15 | convolution fusion | flops 805306368 | bytes 16778240 | tf_op jit(solution)/shard_map/xycoi,xzcoi->yz/dot_general | solution.py:29
  597.5 196.5 %all-reduce.4.cloned.1.call-done = (f32[512,512]{1,0:T(8,128)}, f32[256,256]{1,0:T(8,128)}) async-done(((f32[512,512]{1,0:T(8,128)}, f32[256,256]{1,0:T(8,128)}), (f32[512,512]{1,0:T(8,128)}, f32[256,256]{1,0:T(8,128)})) %all-reduce.4.cloned.1.call-update) | async-done | bytes 1310736 | tf_op jit(solution)/shard_map/psum | solution.py:31
  796.9 11.7 cholesky.158
  823.2 11.9 cholesky.169
  846.6 17.3 %convolution_bitcast_fusion = f32[8,16,2,32,128]{4,3,2,1,0:T(8,128)} fusion(f32[8,16,2,32,512]{4,3,2,1,0:T(8,128)} %param.16, f32[128,512]{1,0:T(8,128)S(1)} %fusion.23), kind=kOutput, calls=%fused_computation.8 | convolution fusion | flops 6442450944 | bytes 21233664 | tf_op jit(solution)/shard_map/xycoi,ia->xycoa/dot_general | solution.py:44
  864.0 54.5 %reduce.13 = f32[4,1048576]{1,0:T(4,128)} reduce(f32[4,1,1048576]{2,1,0:T(1,128)} %all-to-all-done.1, f32[]{:T(128)} %broadcast.120), dimensions={1}, to_apply=%all_to_all.30.reduce_sub_computation | reduce | bytes 33554436 | tf_op jit(solution)/shard_map/all_to_all | solution.py:38
  918.5 76.0 %reshape.48 = f32[512,8,2,16,32]{4,3,2,1,0:T(8,128)} reshape(f32[4,1048576]{1,0:T(4,128)} %reduce.13) | data formatting | bytes 33554432
  994.5 42.8 %copy.85 = f32[8,16,2,32,4,128]{5,0,4,1,3,2:T(8,128)} copy(f32[8,16,2,32,4,128]{3,1,2,0,5,4:T(8,128)} %bitcast.26) | data formatting | bytes 33554432 | tf_op jit(solution)/shard_map/all_to_all | solution.py:38
  1037.3 19.6 %fusion.16 = f32[32,32]{1,0:T(8,128)S(1)} fusion(f32[8,16,2,32,4,128]{5,0,4,1,3,2:T(8,128)} %copy.85), kind=kOutput, calls=%fused_computation.14 | convolution fusion | flops 1610612736 | bytes 16781312 | tf_op jit(solution)/shard_map/xycoi,zycoi->xz/dot_general | solution.py:40
  1057.0 39.5 %all-reduce = (f32[32,32]{1,0:T(8,128)S(1)}, f32[16,16]{1,0:T(8,128)S(1)}) all-reduce(f32[32,32]{1,0:T(8,128)S(1)} %fusion.16, f32[16,16]{1,0:T(8,128)S(1)} %fusion.19), channel_id=1, replica_groups=mesh['fsdp'=8,'mode'=4] {'fsdp','mode'}, use_global_device_ids=true, to_apply=%region_4.8 | all-reduce | flops 1280 | bytes 10240 | tf_op jit(solution)/shard_map/psum | solution.py:39
  1127.7 11.7 cholesky.180
  1151.8 11.7 cholesky.191
  1164.9 10.0 custom-call.25
  1175.2 28.3 %reduce-scatter.3.cloned.1.call-done = f32[4,8,2,32,128]{4,3,2,1,0:T(8,128)} async-done(((f32[16,8,2,32,128]{4,3,2,1,0:T(8,128)}), f32[4,8,2,32,128]{4,3,2,1,0:T(8,128)}) %reduce-scatter.3.cloned.1.call-update) | async-done | bytes 1048592 | tf_op jit(solution)/shard_map/reduce_scatter | solution.py:49
  1211.5 50.3 %reduce-scatter.5.cloned.1.call-done = f32[16,4,8,2,128]{4,0,3,2,1:T(8,128)} async-done(((f32[128,4,8,2,128]{4,0,3,2,1:T(8,128)}), f32[16,4,8,2,128]{4,0,3,2,1:T(8,128)}) %reduce-scatter.5.cloned.1.call-update) | async-done | bytes 524304 | tf_op jit(solution)/shard_map/reduce_scatter | solution.py:56
  (107 shorter events, 97.6 us)
Async XLA Ops:
  7.2 786.8 %copy-start = (f32[512,128]{1,0:T(8,128)S(1)}, f32[512,128]{1,0:T(8,128)}, u32[]{:S(2)}) copy-start(f32[512,128]{1,0:T(8,128)} %param.17) | copy-start | bytes 786436
  124.6 190.3 %all-to-all-start = ((f32[8,1,524288]{2,1,0:T(1,128)}), f32[8,1,524288]{2,1,0:T(1,128)}, u32[]{:S(2)}, u32[]{:S(2)}) async-start(f32[8,1,524288]{2,1,0:T(1,128)} %reshape.45), calls=%async_computation | async-start | bytes 33554432 | tf_op jit(solution)/shard_map/all_to_all | solution.py:34
  314.9 549.1 %all-to-all-start.1 = ((f32[4,1,1048576]{2,1,0:T(1,128)}), f32[4,1,1048576]{2,1,0:T(1,128)}, u32[]{:S(2)}, u32[]{:S(2)}) async-start(f32[4,1,1048576]{2,1,0:T(1,128)} %reshape.47), calls=%async_computation.1 | async-start | bytes 33554432 | tf_op jit(solution)/shard_map/all_to_all | solution.py:38
  322.1 471.9 %all-reduce.4.cloned.1.call-start = ((), (), s32[]{:S(2)}) async-start(), calls=%async_computation.6 | async-start | bytes 2621440 | tf_op jit(solution)/shard_map/psum | solution.py:31
  545.5 657.9 %reduce-scatter.3.cloned.1.call-start = ((), (), s32[]{:S(2)}) async-start(), calls=%async_computation.4 | async-start | bytes 5242880 | tf_op jit(solution)/shard_map/reduce_scatter | solution.py:49
  1037.3 59.2 %copy-start.6 = (f32[16,8]{0,1:T(8,128)S(1)}, f32[16,8]{0,1:T(8,128)}, u32[]{:S(2)}) copy-start(f32[16,8]{0,1:T(8,128)} %param.20) | copy-start | bytes 1540
  1037.3 65.7 %copy-start.5 = (f32[32,16]{0,1:T(8,128)S(1)}, f32[32,16]{0,1:T(8,128)}, u32[]{:S(2)}) copy-start(f32[32,16]{0,1:T(8,128)} %param.19) | copy-start | bytes 6148
  1056.9 69.9 %copy-start.1 = (f32[256,256]{1,0:T(8,128)S(1)}, f32[256,256]{1,0:T(8,128)}, u32[]{:S(2)}) copy-start(f32[256,256]{1,0:T(8,128)} %get-tuple-element.35) | copy-start | bytes 786436
  1057.0 69.9 %copy-start.2 = (f32[256,128]{1,0:T(8,128)S(1)}, f32[256,128]{1,0:T(8,128)}, u32[]{:S(2)}) copy-start(f32[256,128]{1,0:T(8,128)} %param.18) | copy-start | bytes 393220
  1103.0 107.1 %copy-start.4 = (f32[8,16]{1,0:T(8,128)}, f32[8,16]{1,0:T(8,128)S(1)}, u32[]{:S(2)}) copy-start(f32[8,16]{1,0:T(8,128)S(1)} %fusion.64) | copy-start | bytes 1540
  1112.2 97.9 %copy-start.3 = (f32[16,32]{1,0:T(8,128)}, f32[16,32]{1,0:T(8,128)S(1)}, u32[]{:S(2)}) copy-start(f32[16,32]{1,0:T(8,128)S(1)} %fusion.51) | copy-start | bytes 6148
  1126.5 135.2 %reduce-scatter.5.cloned.1.call-start = ((), (), s32[]{:S(2)}) async-start(), calls=%async_computation.5 | async-start | bytes 4718592 | tf_op jit(solution)/shard_map/reduce_scatter | solution.py:56
Sparse Core Ops, SparseCore 0:
  545.6 248.3 all-reduce.3
  1126.7 76.7 reduce-scatter.2
  1210.2 51.5 reduce-scatter.4
where the time goes:
time: 1280 us; the launch traced here: 1270 us
  local copies, waits for them, and re-layouts  408 us (32%)
  waiting for transfers between devices  400 us (31%)
  other arithmetic  210 us (16%)
  matrix products  185 us (14%)
  blocking collectives  39.5 us (3%)
  between operations  14.6 us (1%)
  starting transfers between devices  13.3 us (1%)
    unnamed x21, local copies, waits for them, and re-layouts  312 us
    psum x1, waiting for transfers between devices, shards(): gram_in, gram_y = lax.psum((gram_in_part, gram_y_part), ('fsdp', 'mode'))  197 us
    all_to_all x1, waiting for transfers between devices, shards(): lax.all_to_all(gradient, 'fsdp', split_axis=4, concat_axis=3, tiled=True)  124 us
    another operation x24, other arithmetic, sweeps(): lower_factor = jnp.linalg.cholesky(inner)  56.9 us
    all_to_all x1, other arithmetic, shards(): lax.all_to_all(gradient, 'mode', split_axis=4, concat_axis=0, tiled=True)  54.5 us
    dot_general x1, matrix products, shards(): jnp.einsum('xycoi,xzcoi->yz', gradient, gradient, precision=precise)  51.9 us
    all_to_all x1, other arithmetic, shards(): lax.all_to_all(gradient, 'fsdp', split_axis=4, concat_axis=3, tiled=True)  50.6 us
    reduce_scatter x1, waiting for transfers between devices, shards(): lax.psum_scatter(jnp.einsum('pqcoa,ob->bpqca', partial_core, columns, pre...  50.3 us
  transfers between devices with their start and end apart: 5, of which 4 were waited for; matrix products, arithmetic and copies ran while one was open for 36% of the time, Pallas kernels for 0%

commit v1 on v0

--- a/solution.py
+++ b/solution.py
@@ -1,3 +1,4 @@
+import functools
 import jax
 import jax.numpy as jnp
 from jax import lax
@@ -6,6 +7,17 @@
 I = 512
 SWEEPS = 2
 precise = lax.Precision.HIGHEST
+
+
+def take_chunk_all(unit, device_axis):
+    w_next = jax.lax.axis_size(device_axis)
+    v1 = jnp.split(unit, w_next, 4)
+    local_now = jnp.stack(v1, 0)
+    x_new = jax.lax.all_to_all(local_now, axis_name=device_axis, split_axis=0, concat_axis=0)
+    return jnp.concatenate(x_new, 3)
+
+
+move_the_sample = functools.partial(take_chunk_all, device_axis="fsdp")
 
 
 def sweeps(gram, subspace):
@@ -31,7 +43,7 @@
     gram_in, gram_y = lax.psum((gram_in_part, gram_y_part), ("fsdp", "mode"))
     full_in = sweeps(gram_in, start_in)
     factor_y = sweeps(gram_y, start_y)
-    by_out = lax.all_to_all(gradient, "fsdp", split_axis=4, concat_axis=3, tiled=True)
+    by_out = move_the_sample(gradient)
     gram_out = lax.psum(
         jnp.einsum("xycoi,xycpi->op", by_out, by_out, precision=precise), ("fsdp", "mode")
     )

time: 1280 us -> 1220 us (0.953)
  local copies, waits for them, and re-layouts: 408 us -> 345 us
    psum x1, waiting for transfers between devices: 197 us -> 249 us  [shards(): gram_in, gram_y = lax.psum((gram_in_part, gram_y_part), ('fsdp', 'mode'))]
    all_to_all x1, waiting for transfers between devices: 124 us -> 74 us  [take_chunk_all(): jax.lax.all_to_all(local_now, axis_name=device_axis, split_axis=0, concat...]
    all_to_all x2 -> x1, local copies, waits for them, and re-layouts: 49 us -> 0.51 us  [take_chunk_all(): jax.lax.all_to_all(local_now, axis_name=device_axis, split_axis=0, concat...]
    unnamed x21 -> x30, local copies, waits for them, and re-layouts: 312 us -> 270 us
    reshape x0 -> x1, local copies, waits for them, and re-layouts: none -> 23.5 us  [take_chunk_all(): return jnp.concatenate(x_new, 3)]
  transfers between devices with their start and end apart: 5 -> 5, of which waited for: 4 -> 4; matrix products, arithmetic and copies ran while one was open for 36% -> 37% of each run, Pallas kernels for 0% -> 0%
where the time goes in v1:
time: 1220 us; the launch traced here: 1210 us
  waiting for transfers between devices  402 us (33%)
  local copies, waits for them, and re-layouts  345 us (28%)
  other arithmetic  210 us (17%)
  matrix products  183 us (15%)
  blocking collectives  39.5 us (3%)
  between operations  14.6 us (1%)
  starting transfers between devices  13.7 us (1%)
    unnamed x30, local copies, waits for them, and re-layouts  270 us
    psum x1, waiting for transfers between devices, shards(): gram_in, gram_y = lax.psum((gram_in_part, gram_y_part), ('fsdp', 'mode'))  249 us
    all_to_all x1, waiting for transfers between devices, take_chunk_all(): jax.lax.all_to_all(local_now, axis_name=device_axis, split_axis=0, concat...  74 us
    another operation x24, other arithmetic, sweeps(): lower_factor = jnp.linalg.cholesky(inner)  56.9 us
    all_to_all x1, other arithmetic, shards(): lax.all_to_all(gradient, 'mode', split_axis=4, concat_axis=0, tiled=True)  54.5 us
    dot_general x1, matrix products, shards(): jnp.einsum('xycoi,xzcoi->yz', gradient, gradient, precision=precise)  52.1 us
    reduce_scatter x1, waiting for transfers between devices, shards(): lax.psum_scatter(jnp.einsum('pqcoa,ob->bpqca', partial_core, columns, pre...  50.3 us
    all_to_all x1, other arithmetic, take_chunk_all(): jax.lax.all_to_all(local_now, axis_name=device_axis, split_axis=0, concat...  50.2 us
  transfers between devices with their start and end apart: 5, of which 4 were waited for; matrix products, arithmetic and copies ran while one was open for 37% of the time, Pallas kernels for 0%

profile of v1, /device:TPU:0, one launch (start us, length us, event | category | flops | bytes accessed | tf_op | source)
XLA Modules:
  0.0 1207.6 jit_solution(16921655623508789209)
XLA Ops:
  35.6 25.5 %reshape.53 = f32[8,1,524288]{2,1,0:T(1,128)} reshape(f32[8,8,16,2,32,64]{5,4,3,2,1,0:T(8,128)} %bitcast_dynamic-update-slice_fusion) | data formatting | bytes 33554432
  67.0 50.4 %copy.82 = f32[8,16,2,32,512]{3,1,2,0,4:T(8,128)} copy(f32[8,16,2,32,512]{4,3,2,1,0:T(8,128)} %param.16) | data formatting | bytes 33554432 | tf_op args[0]
  117.4 60.2 %reshape.55 = f32[4,1,1048576]{2,1,0:T(1,128)} reshape(f32[512,8,2,16,32]{4,3,2,1,0:T(8,128)} %bitcast.169) | data formatting | bytes 33554432
  177.6 74.0 %all-to-all-done = f32[8,1,524288]{2,1,0:T(1,128)} async-done(((f32[8,1,524288]{2,1,0:T(1,128)}), f32[8,1,524288]{2,1,0:T(1,128)}, u32[]{:S(2)}, u32[]{:S(2)}) %all-to-all-start) | async-done | bytes 16777248 | tf_op jit(solution)/shard_map/all_to_all | solution.py:16
  259.1 31.6 %fusion.15 = f32[512,512]{1,0:T(8,128)} fusion(f32[8,16,2,32,512]{4,3,2,1,0:T(8,128)} %param.16), kind=kOutput, calls=%fused_computation.22 | convolution fusion | flops 25769803776 | bytes 17825792 | tf_op jit(solution)/shard_map/xycoi,xycoj->ij/dot_general | solution.py:42
  291.2 50.2 %reduce.12 = f32[8,524288]{1,0:T(8,128)} reduce(f32[8,1,524288]{2,1,0:T(1,128)} %all-to-all-done, f32[]{:T(128)} %broadcast.120), dimensions={1}, to_apply=%all_to_all.16.reduce_sub_computation | reduce | bytes 33554436 | tf_op jit(solution)/shard_map/all_to_all | solution.py:16
  341.4 30.2 %reshape.54 = f32[8,8,16,2,32,64]{5,4,3,2,1,0:T(8,128)} reshape(f32[8,524288]{1,0:T(8,128)} %reduce.12) | data formatting | bytes 33554432
  371.6 23.5 %copy.77 = f32[8,16,2,8,32,64]{5,4,3,2,1,0:T(8,128)} copy(f32[8,16,2,8,32,64]{5,4,2,1,0,3:T(8,128)} %bitcast.206) | data formatting | bytes 33554432 | tf_op jit(solution)/shard_map/reshape | solution.py:17
  395.1 34.2 %fusion.18 = f32[256,256]{1,0:T(8,128)} fusion(f32[8,16,2,256,64]{4,3,2,1,0:T(8,128)} %bitcast.205), kind=kOutput, calls=%fused_computation.23 | convolution fusion | flops 12884901888 | bytes 17039360 | tf_op jit(solution)/shard_map/xycoi,xycpi->op/dot_general | solution.py:48
  429.5 52.1 %fusion.24 = f32[16,16]{1,0:T(8,128)S(1)} fusion(f32[8,16,2,32,512]{4,3,2,1,0:T(8,128)} %param.16), kind=kOutput, calls=%fused_computation.25 | convolution fusion | flops 805306368 | bytes 16778240 | tf_op jit(solution)/shard_map/xycoi,xzcoi->yz/dot_general | solution.py:41
  481.6 249.2 %all-reduce.4.cloned.1.call-done = (f32[512,512]{1,0:T(8,128)}, f32[256,256]{1,0:T(8,128)}) async-done(((f32[512,512]{1,0:T(8,128)}, f32[256,256]{1,0:T(8,128)}), (f32[512,512]{1,0:T(8,128)}, f32[256,256]{1,0:T(8,128)})) %all-reduce.4.cloned.1.call-update) | async-done | bytes 1310736 | tf_op jit(solution)/shard_map/psum | solution.py:43
  733.6 11.7 cholesky.158
  759.9 11.9 cholesky.169
  783.4 17.3 %convolution_bitcast_fusion = f32[8,16,2,32,128]{4,3,2,1,0:T(8,128)} fusion(f32[8,16,2,32,512]{4,3,2,1,0:T(8,128)} %param.16, f32[128,512]{1,0:T(8,128)S(1)} %fusion.28), kind=kOutput, calls=%fused_computation.18 | convolution fusion | flops 6442450944 | bytes 21233664 | tf_op jit(solution)/shard_map/xycoi,ia->xycoa/dot_general | solution.py:56
  800.7 54.5 %reduce.13 = f32[4,1048576]{1,0:T(4,128)} reduce(f32[4,1,1048576]{2,1,0:T(1,128)} %all-to-all-done.1, f32[]{:T(128)} %broadcast.120), dimensions={1}, to_apply=%all_to_all.17.reduce_sub_computation | reduce | bytes 33554436 | tf_op jit(solution)/shard_map/all_to_all | solution.py:50
  855.2 76.0 %reshape.56 = f32[512,8,2,16,32]{4,3,2,1,0:T(8,128)} reshape(f32[4,1048576]{1,0:T(4,128)} %reduce.13) | data formatting | bytes 33554432
  931.2 42.8 %copy.83 = f32[8,16,2,32,4,128]{5,0,4,1,3,2:T(8,128)} copy(f32[8,16,2,32,4,128]{3,1,2,0,5,4:T(8,128)} %bitcast.32) | data formatting | bytes 33554432 | tf_op jit(solution)/shard_map/all_to_all | solution.py:50
  974.0 19.6 %fusion.21 = f32[32,32]{1,0:T(8,128)S(1)} fusion(f32[8,16,2,32,4,128]{5,0,4,1,3,2:T(8,128)} %copy.83), kind=kOutput, calls=%fused_computation.24 | convolution fusion | flops 1610612736 | bytes 16781312 | tf_op jit(solution)/shard_map/xycoi,zycoi->xz/dot_general | solution.py:52
  993.7 39.5 %all-reduce = (f32[32,32]{1,0:T(8,128)S(1)}, f32[16,16]{1,0:T(8,128)S(1)}) all-reduce(f32[32,32]{1,0:T(8,128)S(1)} %fusion.21, f32[16,16]{1,0:T(8,128)S(1)} %fusion.24), channel_id=1, replica_groups=mesh['fsdp'=8,'mode'=4] {'fsdp','mode'}, use_global_device_ids=true, to_apply=%region_4.8 | all-reduce | flops 1280 | bytes 10240 | tf_op jit(solution)/shard_map/psum | solution.py:51
  1064.4 11.7 cholesky.180
  1088.5 11.7 cholesky.191
  1101.5 10.0 custom-call.25
  1111.9 28.3 %reduce-scatter.3.cloned.1.call-done = f32[4,8,2,32,128]{4,3,2,1,0:T(8,128)} async-done(((f32[16,8,2,32,128]{4,3,2,1,0:T(8,128)}), f32[4,8,2,32,128]{4,3,2,1,0:T(8,128)}) %reduce-scatter.3.cloned.1.call-update) | async-done | bytes 1048592 | tf_op jit(solution)/shard_map/reduce_scatter | solution.py:61
  1148.2 50.3 %reduce-scatter.5.cloned.1.call-done = f32[16,4,8,2,128]{4,0,3,2,1:T(8,128)} async-done(((f32[128,4,8,2,128]{4,0,3,2,1:T(8,128)}), f32[16,4,8,2,128]{4,0,3,2,1:T(8,128)}) %reduce-scatter.5.cloned.1.call-update) | async-done | bytes 524304 | tf_op jit(solution)/shard_map/reduce_scatter | solution.py:68
  (117 shorter events, 126.4 us)
Async XLA Ops:
  7.2 723.6 %copy-start = (f32[512,128]{1,0:T(8,128)S(1)}, f32[512,128]{1,0:T(8,128)}, u32[]{:S(2)}) copy-start(f32[512,128]{1,0:T(8,128)} %param.17) | copy-start | bytes 786436
  7.2 11.4 copy-start.1
  61.1 190.5 %all-to-all-start = ((f32[8,1,524288]{2,1,0:T(1,128)}), f32[8,1,524288]{2,1,0:T(1,128)}, u32[]{:S(2)}, u32[]{:S(2)}) async-start(f32[8,1,524288]{2,1,0:T(1,128)} %reshape.53), calls=%async_computation | async-start | bytes 33554432 | tf_op jit(solution)/shard_map/all_to_all | solution.py:16
  251.6 549.1 %all-to-all-start.1 = ((f32[4,1,1048576]{2,1,0:T(1,128)}), f32[4,1,1048576]{2,1,0:T(1,128)}, u32[]{:S(2)}, u32[]{:S(2)}) async-start(f32[4,1,1048576]{2,1,0:T(1,128)} %reshape.55), calls=%async_computation.1 | async-start | bytes 33554432 | tf_op jit(solution)/shard_map/all_to_all | solution.py:50
  258.6 472.1 %all-reduce.4.cloned.1.call-start = ((), (), s32[]{:S(2)}) async-start(), calls=%async_computation.6 | async-start | bytes 2621440 | tf_op jit(solution)/shard_map/psum | solution.py:43
  429.4 710.7 %reduce-scatter.3.cloned.1.call-start = ((), (), s32[]{:S(2)}) async-start(), calls=%async_computation.4 | async-start | bytes 5242880 | tf_op jit(solution)/shard_map/reduce_scatter | solution.py:61
  974.0 59.2 %copy-start.7 = (f32[16,8]{0,1:T(8,128)S(1)}, f32[16,8]{0,1:T(8,128)}, u32[]{:S(2)}) copy-start(f32[16,8]{0,1:T(8,128)} %param.20) | copy-start | bytes 1540
  974.0 65.7 %copy-start.6 = (f32[32,16]{0,1:T(8,128)S(1)}, f32[32,16]{0,1:T(8,128)}, u32[]{:S(2)}) copy-start(f32[32,16]{0,1:T(8,128)} %param.19) | copy-start | bytes 6148
  993.7 69.9 %copy-start.2 = (f32[256,256]{1,0:T(8,128)S(1)}, f32[256,256]{1,0:T(8,128)}, u32[]{:S(2)}) copy-start(f32[256,256]{1,0:T(8,128)} %get-tuple-element.35) | copy-start | bytes 786436
  993.7 69.9 %copy-start.3 = (f32[256,128]{1,0:T(8,128)S(1)}, f32[256,128]{1,0:T(8,128)}, u32[]{:S(2)}) copy-start(f32[256,128]{1,0:T(8,128)} %param.18) | copy-start | bytes 393220
  1039.7 107.1 %copy-start.5 = (f32[8,16]{1,0:T(8,128)}, f32[8,16]{1,0:T(8,128)S(1)}, u32[]{:S(2)}) copy-start(f32[8,16]{1,0:T(8,128)S(1)} %fusion.69) | copy-start | bytes 1540
  1048.9 97.9 %copy-start.4 = (f32[16,32]{1,0:T(8,128)}, f32[16,32]{1,0:T(8,128)S(1)}, u32[]{:S(2)}) copy-start(f32[16,32]{1,0:T(8,128)S(1)} %fusion.56) | copy-start | bytes 6148
  1063.2 135.3 %reduce-scatter.5.cloned.1.call-start = ((), (), s32[]{:S(2)}) async-start(), calls=%async_computation.5 | async-start | bytes 4718592 | tf_op jit(solution)/shard_map/reduce_scatter | solution.py:68
Sparse Core Ops, SparseCore 0:
  429.5 301.1 all-reduce.3
  1063.4 76.7 reduce-scatter.2
  1146.9 51.5 reduce-scatter.4
